TPU v7x, 256 devices: a whole 4x4x8 slice. The times are simulated.
256 devices in a mesh: layer: 16 (over z_hi, x, core), sub: 16 (over y, z_lo).
Axes of the slice: x: 4, y: 4, z: 8 (z_hi: 2, z_lo: 4; z = z_hi * 4 + z_lo), core: 2. Of those that a mesh axis runs over, the one named last changes fastest.
Arguments:
- screens: float32 [16, 7, 2048, 640], P('layer', None, None, 'sub'), may hold values from -4 to 4
- new_columns: float32 [10, 16, 2048, 8], P(None, 'layer'), may hold values from -4 to 4
- col_block: int32 [10, 16], P(None, 'layer'), may hold values from 240 to 319
- shift_x: int32 [10, 16, 6], P(None, 'layer'), may hold values from -40 to 40, as said below
- shift_y: int32 [10, 16, 6], P(None, 'layer'), may hold values from -40 to 40, as said below
- valid: int32 [80, 80], P('layer', 'sub'), may hold values 0 or 1
- recon: bfloat16 [6, 2, 80, 80, 5376], P(None, None, 'layer', 'sub'), may hold values from -0.0234375 to 0.0234375
Outputs:
- slopes: float32 [10, 6, 2, 80, 80], P(None, None, None, 'layer', 'sub')
- commands: float32 [10, 5376], replicated
Inputs may be any that keep to these rules, and one draw needn't show every extreme that they name: `shift_x`: column shifts reach both -40 and 40 in every draw. `shift_y`: row shifts reach both -40 and 40 in every draw.
All inputs are finite; a program needn't handle non-finite values. No bound on the sum of `valid` on one device may be relied on, other than what follows from the above.
Results may differ from a plain program's by a relative error of at most 0.0029.
Values sent between devices are 32-bit elements; how exact they have to be, the bound alone decides.
No kernel may reach another device: no remote copies, remote signals or barrier semaphores. Data moves between devices by JAX's collectives and lax.ppermute only.
A program may use at most 64 MiB of HBM per device.

v0:
```python
import math
import jax
import jax.numpy as jnp
from jax import lax
from jax.sharding import PartitionSpec as P

FFT_LEN = 16
ACTS = 5376
HALO = 40
NEW_COLS = 8
PUP = 640
PUP_TURN = 3
ROW0 = 704


def extended_2(block, sides, width):
    for axis, dim in sides:
        count = lax.axis_size(axis)
        forward = [(i, i + 1) for i in range(count - 1)]
        forward.append((count - 1, 0))
        backward = [(target, source) for source, target in forward]
        low = lax.ppermute(
            lax.slice_in_dim(block, block.shape[dim] - width, None, axis=dim), axis, forward
        )
        high = lax.ppermute(lax.slice_in_dim(block, 0, width, axis=dim), axis, backward)
        block = jnp.concatenate([low, block, high], axis=dim)
    return block


def lenslet_slopes(phase, valid, fft_len):
    stars, rows, cols = phase.shape
    subs_r, subs_c = valid.shape
    pix = rows // subs_r
    tiles = phase.reshape(stars, subs_r, pix, subs_c, pix)
    tiles = jnp.transpose(tiles, (2, 4, 0, 1, 3)).reshape(pix, pix, stars * subs_r * subs_c)
    freq = jnp.arange(fft_len).astype(jnp.float32)
    place = jnp.arange(pix).astype(jnp.float32)
    angle = 2.0 * math.pi / fft_len * freq[:, None] * place[None, :]
    cosine = jnp.cos(angle)
    sine = -jnp.sin(angle)
    real_part = jnp.cos(tiles)
    imag_part = jnp.sin(tiles)
    highest = lax.Precision.HIGHEST

    def along_rows(mat, field):
        return jnp.einsum("kn,nms->kms", mat, field, precision=highest)

    def along_cols(field, mat):
        return jnp.einsum("kms,qm->kqs", field, mat, precision=highest)

    first_re = along_rows(cosine, real_part) - along_rows(sine, imag_part)
    first_im = along_rows(cosine, imag_part) + along_rows(sine, real_part)
    spot_re = along_cols(first_re, cosine) - along_cols(first_im, sine)
    spot_im = along_cols(first_re, sine) + along_cols(first_im, cosine)
    power = spot_re * spot_re + spot_im * spot_im
    centred = ((jnp.arange(fft_len) + fft_len // 2) % fft_len - fft_len // 2).astype(jnp.float32)
    total = jnp.sum(power, axis=(0, 1))
    along_x = jnp.sum(power * centred[None, :, None], axis=(0, 1)) / total
    along_y = jnp.sum(power * centred[:, None, None], axis=(0, 1)) / total
    result = jnp.stack([along_x, along_y]).reshape(2, stars, subs_r, subs_c)
    return jnp.transpose(result, (1, 0, 2, 3)) * valid.astype(jnp.float32)[None, None]


def place_columns(strips, fresh, block, owner, width):
    column = block * NEW_COLS
    turn = column // PUP
    start = column % PUP - owner * width
    inside = (start >= 0) & (start < width)
    offset = jnp.clip(start, 0, width - NEW_COLS)
    placed = lax.dynamic_update_slice(strips, fresh[None], (turn, jnp.int32(0), offset))
    return jnp.where(inside, placed, strips)


def cut_window(extended, step_x, step_y, width):
    return lax.dynamic_slice(extended, (HALO + step_y, HALO + step_x), (PUP, width))


def local(screens, new_columns, col_block, shift_x, shift_y, valid, recon):
    width = screens.shape[3]
    owner = lax.axis_index("sub")
    last = lax.axis_size("sub") - 1
    matrix = recon.reshape(-1, ACTS)

    def advance(strips, inputs):
        fresh, blocks, step_x, step_y = inputs
        strips = jax.vmap(lambda s, f, b: place_columns(s, f, b, owner, width))(
            strips, fresh, blocks
        )
        band = strips[:, PUP_TURN - 1 : PUP_TURN + 2, ROW0 - HALO : ROW0 + PUP + HALO, :]
        before = band[:, 0]
        core = band[:, 1]
        after = band[:, 2]
        tail_cols = jnp.where(owner == last, before, core)
        head_cols = jnp.where(owner == 0, after, core)
        rims = jnp.concatenate([head_cols, tail_cols], axis=2)
        padded = extended_2(rims, (("sub", 2),), HALO)
        extended = jnp.concatenate(
            [padded[:, :, :HALO], core, padded[:, :, padded.shape[2] - HALO :]], axis=2
        )
        window = jax.vmap(
            jax.vmap(lambda e, x, y: cut_window(e, x, y, width), in_axes=(None, 0, 0))
        )(extended, step_x, step_y)
        summed = lax.all_to_all(window, "layer", split_axis=2, concat_axis=0, tiled=True)
        phase = jnp.sum(summed, axis=0)
        slopes = lenslet_slopes(phase, valid, FFT_LEN)
        flat = slopes.astype(jnp.bfloat16).reshape(-1)
        partial_cmd = jnp.dot(flat, matrix, preferred_element_type=jnp.float32)
        command = lax.psum(partial_cmd, ("layer", "sub"))
        return (strips, (slopes, command))

    final, (slopes, commands) = lax.scan(
        advance, screens, (new_columns, col_block, shift_x, shift_y)
    )
    return (slopes, commands)


def solution(mesh):
    return jax.shard_map(
        local,
        mesh=mesh,
        in_specs=(
            P("layer", None, None, "sub"),
            P(None, "layer", None, None),
            P(None, "layer"),
            P(None, "layer", None),
            P(None, "layer", None),
            P("layer", "sub"),
            P(None, None, "layer", "sub", None),
        ),
        out_specs=(P(None, None, None, "layer", "sub"), P()),
        check_vma=False,
    )
```

profile of v0, /device:TPU:1, one launch (start us, length us, event | category | flops | bytes accessed | tf_op | source)
XLA Modules:
  0.0 1927.3 jit_solution(1306856155262718636)
XLA Ops:
  5.4 7.2 reshape.421
  17.1 1908.1 %while.21 = (s32[]{:T(128)}, f32[1,7,2048,40]{3,2,1,0:T(8,128)}, f32[10,6,2,5,5]{1,2,4,3,0:T(2,128)}, f32[10,5376]{1,0:T(8,128)}, s32[10,1]{0,1:T(1,128)S(1)}, /...) while((s32[]{:T(128)}, f32[1,7,2048,40]{3,2,1,0:T(8,128)}, ...), condition=%wide.region_7.8_spmd, body=%wide.region_0.7_spmd.sunk | while | flops 26182216 | bytes 32231552 | solution.py:111
  27.7 7.2 select_n.167
  50.5 8.9 collective-permute-done.1
  60.6 12.9 while.22
  87.0 11.1 all-to-all-start
  98.1 18.1 all-to-all-done
  137.5 76.0 %psum.12 = f32[1,5376]{1,0:T(1,128)S(1)} all-reduce(f32[1,5376]{1,0:T(1,128)S(1)} %fusion.108), channel_id=1, replica_groups=mesh['layer'=16,'sub'=16] {'layer','sub'}, use_global_device_ids=true, to_apply=%region_6.6 | all-reduce | flops 5376 | bytes 43008 | tf_op jit(solution)/shard_map/while/body/eval_jaxpr/psum | solution.py:108
  244.5 9.2 collective-permute-done.1
  255.0 12.9 while.22
  286.2 15.7 all-to-all-done
  323.1 80.1 %psum.12 = f32[1,5376]{1,0:T(1,128)S(1)} all-reduce(f32[1,5376]{1,0:T(1,128)S(1)} %fusion.108), channel_id=1, replica_groups=mesh['layer'=16,'sub'=16] {'layer','sub'}, use_global_device_ids=true, to_apply=%region_6.6 | all-reduce | flops 5376 | bytes 43008 | tf_op jit(solution)/shard_map/while/body/eval_jaxpr/psum | solution.py:108
  416.2 7.2 select_n.167
  427.3 7.7 collective-permute-done
  435.0 7.4 collective-permute-done.1
  443.7 12.9 while.22
  476.1 15.7 all-to-all-done
  513.0 80.2 %psum.12 = f32[1,5376]{1,0:T(1,128)S(1)} all-reduce(f32[1,5376]{1,0:T(1,128)S(1)} %fusion.108), channel_id=1, replica_groups=mesh['layer'=16,'sub'=16] {'layer','sub'}, use_global_device_ids=true, to_apply=%region_6.6 | all-reduce | flops 5376 | bytes 43008 | tf_op jit(solution)/shard_map/while/body/eval_jaxpr/psum | solution.py:108
  606.1 7.2 select_n.167
  617.2 8.4 collective-permute-done
  633.7 12.9 while.22
  666.1 15.7 all-to-all-done
  703.0 80.1 %psum.12 = f32[1,5376]{1,0:T(1,128)S(1)} all-reduce(f32[1,5376]{1,0:T(1,128)S(1)} %fusion.108), channel_id=1, replica_groups=mesh['layer'=16,'sub'=16] {'layer','sub'}, use_global_device_ids=true, to_apply=%region_6.6 | all-reduce | flops 5376 | bytes 43008 | tf_op jit(solution)/shard_map/while/body/eval_jaxpr/psum | solution.py:108
  796.1 7.2 select_n.167
  814.1 8.3 collective-permute-done.1
  823.7 12.9 while.22
  856.0 15.7 all-to-all-done
  893.0 80.1 %psum.12 = f32[1,5376]{1,0:T(1,128)S(1)} all-reduce(f32[1,5376]{1,0:T(1,128)S(1)} %fusion.108), channel_id=1, replica_groups=mesh['layer'=16,'sub'=16] {'layer','sub'}, use_global_device_ids=true, to_apply=%region_6.6 | all-reduce | flops 5376 | bytes 43008 | tf_op jit(solution)/shard_map/while/body/eval_jaxpr/psum | solution.py:108
  1004.1 8.2 collective-permute-done.1
  1013.5 12.9 while.22
  1046.0 15.7 all-to-all-done
  1082.9 80.1 %psum.12 = f32[1,5376]{1,0:T(1,128)S(1)} all-reduce(f32[1,5376]{1,0:T(1,128)S(1)} %fusion.108), channel_id=1, replica_groups=mesh['layer'=16,'sub'=16] {'layer','sub'}, use_global_device_ids=true, to_apply=%region_6.6 | all-reduce | flops 5376 | bytes 43008 | tf_op jit(solution)/shard_map/while/body/eval_jaxpr/psum | solution.py:108
  1194.0 8.3 collective-permute-done.1
  1203.6 12.9 while.22
  1235.9 15.7 all-to-all-done
  1272.9 80.2 %psum.12 = f32[1,5376]{1,0:T(1,128)S(1)} all-reduce(f32[1,5376]{1,0:T(1,128)S(1)} %fusion.108), channel_id=1, replica_groups=mesh['layer'=16,'sub'=16] {'layer','sub'}, use_global_device_ids=true, to_apply=%region_6.6 | all-reduce | flops 5376 | bytes 43008 | tf_op jit(solution)/shard_map/while/body/eval_jaxpr/psum | solution.py:108
  1384.0 7.4 collective-permute-done.1
  1392.6 12.9 while.22
  1425.9 15.7 all-to-all-done
  1462.9 80.1 %psum.12 = f32[1,5376]{1,0:T(1,128)S(1)} all-reduce(f32[1,5376]{1,0:T(1,128)S(1)} %fusion.108), channel_id=1, replica_groups=mesh['layer'=16,'sub'=16] {'layer','sub'}, use_global_device_ids=true, to_apply=%region_6.6 | all-reduce | flops 5376 | bytes 43008 | tf_op jit(solution)/shard_map/while/body/eval_jaxpr/psum | solution.py:108
  1573.9 8.2 collective-permute-done.1
  1583.4 12.9 while.22
  1615.8 15.7 all-to-all-done
  1652.8 80.2 %psum.12 = f32[1,5376]{1,0:T(1,128)S(1)} all-reduce(f32[1,5376]{1,0:T(1,128)S(1)} %fusion.108), channel_id=1, replica_groups=mesh['layer'=16,'sub'=16] {'layer','sub'}, use_global_device_ids=true, to_apply=%region_6.6 | all-reduce | flops 5376 | bytes 43008 | tf_op jit(solution)/shard_map/while/body/eval_jaxpr/psum | solution.py:108
  1763.9 7.5 collective-permute-done.1
  1772.6 12.9 while.22
  1805.8 15.7 all-to-all-done
  1842.7 80.2 %psum.12 = f32[1,5376]{1,0:T(1,128)S(1)} all-reduce(f32[1,5376]{1,0:T(1,128)S(1)} %fusion.108), channel_id=1, replica_groups=mesh['layer'=16,'sub'=16] {'layer','sub'}, use_global_device_ids=true, to_apply=%region_6.6 | all-reduce | flops 5376 | bytes 43008 | tf_op jit(solution)/shard_map/while/body/eval_jaxpr/psum | solution.py:108
  (786 shorter events, 809.5 us)
Async XLA Ops:
  5.4 7.2 copy-start.1
  12.6 4.3 copy-start.5
  12.6 4.4 copy-start.6
  12.6 4.5 copy-start.4
  12.6 4.5 copy-start.2
  12.6 4.5 copy-start.3
  12.7 4.5 copy-start.7
  36.2 14.2 collective-permute-start
  43.1 16.2 collective-permute-start.1
  87.0 29.2 %all-to-all-start = ((f32[16,1,9600]{2,1,0:T(1,128)}), f32[16,1,9600]{2,1,0:T(1,128)S(1)}, u32[]{:S(2)}, u32[]{:S(2)}) async-start(f32[16,1,9600]{2,1,0:T(1,128)} %reshape.457), calls=%async_computation | async-start | bytes 1228800 | tf_op jit(solution)/shard_map/while/body/eval_jaxpr/all_to_all | solution.py:103
  127.2 9.8 copy-start
  234.9 9.7 collective-permute-start
  236.1 17.6 collective-permute-start.1
  281.4 20.5 %all-to-all-start = ((f32[16,1,9600]{2,1,0:T(1,128)}), f32[16,1,9600]{2,1,0:T(1,128)S(1)}, u32[]{:S(2)}, u32[]{:S(2)}) async-start(f32[16,1,9600]{2,1,0:T(1,128)} %reshape.457), calls=%async_computation | async-start | bytes 1228800 | tf_op jit(solution)/shard_map/while/body/eval_jaxpr/all_to_all | solution.py:103
  312.8 9.8 copy-start
  424.7 10.3 collective-permute-start
  426.2 16.2 collective-permute-start.1
  470.1 21.7 %all-to-all-start = ((f32[16,1,9600]{2,1,0:T(1,128)}), f32[16,1,9600]{2,1,0:T(1,128)S(1)}, u32[]{:S(2)}, u32[]{:S(2)}) async-start(f32[16,1,9600]{2,1,0:T(1,128)} %reshape.457), calls=%async_computation | async-start | bytes 1228800 | tf_op jit(solution)/shard_map/while/body/eval_jaxpr/all_to_all | solution.py:103
  502.7 9.8 copy-start
  614.6 11.0 collective-permute-start
  616.1 16.3 collective-permute-start.1
  660.1 21.6 %all-to-all-start = ((f32[16,1,9600]{2,1,0:T(1,128)}), f32[16,1,9600]{2,1,0:T(1,128)S(1)}, u32[]{:S(2)}, u32[]{:S(2)}) async-start(f32[16,1,9600]{2,1,0:T(1,128)} %reshape.457), calls=%async_computation | async-start | bytes 1228800 | tf_op jit(solution)/shard_map/while/body/eval_jaxpr/all_to_all | solution.py:103
  692.7 9.8 copy-start
  804.6 9.5 collective-permute-start
  806.1 16.3 collective-permute-start.1
  850.1 21.7 %all-to-all-start = ((f32[16,1,9600]{2,1,0:T(1,128)}), f32[16,1,9600]{2,1,0:T(1,128)S(1)}, u32[]{:S(2)}, u32[]{:S(2)}) async-start(f32[16,1,9600]{2,1,0:T(1,128)} %reshape.457), calls=%async_computation | async-start | bytes 1228800 | tf_op jit(solution)/shard_map/while/body/eval_jaxpr/all_to_all | solution.py:103
  882.7 9.8 copy-start
  994.5 9.5 collective-permute-start
  996.0 16.3 collective-permute-start.1
  1040.0 21.7 %all-to-all-start = ((f32[16,1,9600]{2,1,0:T(1,128)}), f32[16,1,9600]{2,1,0:T(1,128)S(1)}, u32[]{:S(2)}, u32[]{:S(2)}) async-start(f32[16,1,9600]{2,1,0:T(1,128)} %reshape.457), calls=%async_computation | async-start | bytes 1228800 | tf_op jit(solution)/shard_map/while/body/eval_jaxpr/all_to_all | solution.py:103
  1072.6 9.8 copy-start
  1184.4 9.5 collective-permute-start
  1186.0 16.3 collective-permute-start.1
  1230.0 21.6 %all-to-all-start = ((f32[16,1,9600]{2,1,0:T(1,128)}), f32[16,1,9600]{2,1,0:T(1,128)S(1)}, u32[]{:S(2)}, u32[]{:S(2)}) async-start(f32[16,1,9600]{2,1,0:T(1,128)} %reshape.457), calls=%async_computation | async-start | bytes 1228800 | tf_op jit(solution)/shard_map/while/body/eval_jaxpr/all_to_all | solution.py:103
  1262.5 9.8 copy-start
  1374.4 9.5 collective-permute-start
  1376.0 15.4 collective-permute-start.1
  1419.1 22.6 %all-to-all-start = ((f32[16,1,9600]{2,1,0:T(1,128)}), f32[16,1,9600]{2,1,0:T(1,128)S(1)}, u32[]{:S(2)}, u32[]{:S(2)}) async-start(f32[16,1,9600]{2,1,0:T(1,128)} %reshape.457), calls=%async_computation | async-start | bytes 1228800 | tf_op jit(solution)/shard_map/while/body/eval_jaxpr/all_to_all | solution.py:103
  1452.6 9.8 copy-start
  1564.4 9.5 collective-permute-start
  1565.9 16.3 collective-permute-start.1
  1609.8 21.7 %all-to-all-start = ((f32[16,1,9600]{2,1,0:T(1,128)}), f32[16,1,9600]{2,1,0:T(1,128)S(1)}, u32[]{:S(2)}, u32[]{:S(2)}) async-start(f32[16,1,9600]{2,1,0:T(1,128)} %reshape.457), calls=%async_computation | async-start | bytes 1228800 | tf_op jit(solution)/shard_map/while/body/eval_jaxpr/all_to_all | solution.py:103
  1642.4 9.8 copy-start
  1754.3 9.5 collective-permute-start
  1755.9 15.4 collective-permute-start.1
  1799.0 22.5 %all-to-all-start = ((f32[16,1,9600]{2,1,0:T(1,128)}), f32[16,1,9600]{2,1,0:T(1,128)S(1)}, u32[]{:S(2)}, u32[]{:S(2)}) async-start(f32[16,1,9600]{2,1,0:T(1,128)} %reshape.457), calls=%async_computation | async-start | bytes 1228800 | tf_op jit(solution)/shard_map/while/body/eval_jaxpr/all_to_all | solution.py:103
  1832.4 9.8 copy-start
where the time goes:
time: 1940 us; the launch traced here: 1930 us
  blocking collectives  797 us (41%)
  local copies, waits for them, and re-layouts  469 us (24%)
  waiting for transfers between devices  311 us (16%)
  other arithmetic  196 us (10%)
  starting transfers between devices  85.9 us (4%)
  matrix products  44.6 us (2%)
  loops' own time  23.6 us (1%)
    psum x10, blocking collectives, advance(): command = lax.psum(partial_cmd, ('layer', 'sub'))  797 us
    all_to_all x10, waiting for transfers between devices, advance(): lax.all_to_all(window, 'layer', split_axis=2, concat_axis=0, tiled=True)  159 us
    gather x180, local copies, waits for them, and re-layouts  127 us
    while x60, local copies, waits for them, and re-layouts  99.3 us
    ppermute x10, waiting for transfers between devices, extended_2(): lax.ppermute(lax.slice_in_dim(block, block.shape[dim] - width, None, axis...  80.3 us
    select_n x10, local copies, waits for them, and re-layouts, place_columns(): return jnp.where(inside, placed, strips)  72.2 us
    while x20, other arithmetic  71.1 us
    ppermute x10, waiting for transfers between devices, extended_2(): lax.ppermute(lax.slice_in_dim(block, 0, width, axis=dim), axis, backward)  70.9 us
  transfers between devices with their start and end apart: 30, of which 30 were waited for; matrix products, arithmetic and copies ran while one was open for 1% of the time, Pallas kernels for 0%

commit v1 on v0

--- a/solution.py
+++ b/solution.py
@@ -105,7 +105,7 @@
         slopes = lenslet_slopes(phase, valid, FFT_LEN)
         flat = slopes.astype(jnp.bfloat16).reshape(-1)
         partial_cmd = jnp.dot(flat, matrix, preferred_element_type=jnp.float32)
-        command = lax.psum(partial_cmd, ("layer", "sub"))
+        command = jnp.sum(lax.all_gather(partial_cmd, ("layer", "sub")), axis=0)
         return (strips, (slopes, command))
 
     final, (slopes, commands) = lax.scan(

time: 1940 us -> 8360 us (4.31)
  waiting for transfers between devices: 311 us -> 7390 us
  blocking collectives: 797 us -> 0 us
    all_gather x0 -> x10, waiting for transfers between devices: none -> 7110 us  [advance(): command = jnp.sum(lax.all_gather(partial_cmd, ('layer', 'sub')), axis=0)]
    psum x10 -> x0, blocking collectives: 797 us -> none  [advance(): command = lax.psum(partial_cmd, ('layer', 'sub'))]
  transfers between devices with their start and end apart: 30 -> 40, of which waited for: 30 -> 40; matrix products, arithmetic and copies ran while one was open for 1% -> 0% of each run, Pallas kernels for 0% -> 0%
where the time goes in v1:
time: 8360 us; the launch traced here: 8350 us
  waiting for transfers between devices  7390 us (88%)
  local copies, waits for them, and re-layouts  459 us (5%)
  other arithmetic  250 us (3%)
  starting transfers between devices  164 us (2%)
    all_gather x10, waiting for transfers between devices, advance(): command = jnp.sum(lax.all_gather(partial_cmd, ('layer', 'sub')), axis=0)  7110 us
  transfers between devices with their start and end apart: 40, of which 40 were waited for; matrix products, arithmetic and copies ran while one was open for 0% of the time, Pallas kernels for 0%

profile of v1, /device:TPU:1, one launch (start us, length us, event | category | flops | bytes accessed | tf_op | source)
XLA Modules:
  0.0 8350.8 jit_solution(16508033242063637443)
XLA Ops:
  23.6 8318.3 %while.21 = (s32[]{:T(128)}, f32[1,7,2048,40]{3,2,1,0:T(8,128)}, f32[10,6,2,5,5]{1,2,4,3,0:T(2,128)}, f32[10,5376]{1,0:T(8,128)}, s32[10,1]{0,1:T(1,128)S(1)}, /...) while((s32[]{:T(128)}, f32[1,7,2048,40]{3,2,1,0:T(8,128)}, ...), condition=%wide.region_7.8_spmd, body=%wide.region_0.7_spmd.sunk | while | flops 27547720 | bytes 54337708 | solution.py:111
  56.8 8.9 collective-permute-done.1
  66.9 11.9 while.22
  92.4 11.1 all-to-all-start
  103.6 18.0 all-to-all-done
  144.2 709.2 %all-gather.6.cloned.1.call-done = f32[256,1,5376]{2,1,0:T(1,128)} async-done(((f32[1,1,5376]{2,1,0:T(1,128)}), f32[256,1,5376]{2,1,0:T(1,128)}) %all-gather.6.cloned.1.call-update) | async-done | bytes 5505040 | tf_op jit(solution)/shard_map/while/body/eval_jaxpr/all_gather | solution.py:108
  883.8 7.7 collective-permute-done
  896.1 11.9 while.22
  921.6 13.0 all-to-all-start
  934.7 16.0 all-to-all-done
  973.4 711.3 %all-gather.6.cloned.1.call-done = f32[256,1,5376]{2,1,0:T(1,128)} async-done(((f32[1,1,5376]{2,1,0:T(1,128)}), f32[256,1,5376]{2,1,0:T(1,128)}) %all-gather.6.cloned.1.call-update) | async-done | bytes 5505040 | tf_op jit(solution)/shard_map/while/body/eval_jaxpr/all_gather | solution.py:108
  1715.1 7.8 collective-permute-done
  1727.4 11.9 while.22
  1752.8 13.0 all-to-all-start
  1766.0 16.0 all-to-all-done
  1804.6 711.3 %all-gather.6.cloned.1.call-done = f32[256,1,5376]{2,1,0:T(1,128)} async-done(((f32[1,1,5376]{2,1,0:T(1,128)}), f32[256,1,5376]{2,1,0:T(1,128)}) %all-gather.6.cloned.1.call-update) | async-done | bytes 5505040 | tf_op jit(solution)/shard_map/while/body/eval_jaxpr/all_gather | solution.py:108
  2558.6 11.9 while.22
  2584.1 13.0 all-to-all-start
  2597.2 16.0 all-to-all-done
  2635.9 711.3 %all-gather.6.cloned.1.call-done = f32[256,1,5376]{2,1,0:T(1,128)} async-done(((f32[1,1,5376]{2,1,0:T(1,128)}), f32[256,1,5376]{2,1,0:T(1,128)}) %all-gather.6.cloned.1.call-update) | async-done | bytes 5505040 | tf_op jit(solution)/shard_map/while/body/eval_jaxpr/all_gather | solution.py:108
  3377.6 7.8 collective-permute-done
  3389.8 11.9 while.22
  3415.3 12.5 all-to-all-start
  3427.9 15.4 all-to-all-done
  3465.9 712.7 %all-gather.6.cloned.1.call-done = f32[256,1,5376]{2,1,0:T(1,128)} async-done(((f32[1,1,5376]{2,1,0:T(1,128)}), f32[256,1,5376]{2,1,0:T(1,128)}) %all-gather.6.cloned.1.call-update) | async-done | bytes 5505040 | tf_op jit(solution)/shard_map/while/body/eval_jaxpr/all_gather | solution.py:108
  4208.9 7.7 collective-permute-done
  4221.2 11.9 while.22
  4246.7 13.0 all-to-all-start
  4259.8 16.0 all-to-all-done
  4298.5 711.3 %all-gather.6.cloned.1.call-done = f32[256,1,5376]{2,1,0:T(1,128)} async-done(((f32[1,1,5376]{2,1,0:T(1,128)}), f32[256,1,5376]{2,1,0:T(1,128)}) %all-gather.6.cloned.1.call-update) | async-done | bytes 5505040 | tf_op jit(solution)/shard_map/while/body/eval_jaxpr/all_gather | solution.py:108
  5040.2 7.7 collective-permute-done
  5052.5 11.9 while.22
  5077.9 13.0 all-to-all-start
  5091.1 16.0 all-to-all-done
  5129.7 711.3 %all-gather.6.cloned.1.call-done = f32[256,1,5376]{2,1,0:T(1,128)} async-done(((f32[1,1,5376]{2,1,0:T(1,128)}), f32[256,1,5376]{2,1,0:T(1,128)}) %all-gather.6.cloned.1.call-update) | async-done | bytes 5505040 | tf_op jit(solution)/shard_map/while/body/eval_jaxpr/all_gather | solution.py:108
  5871.4 7.7 collective-permute-done
  5883.7 11.9 while.22
  5909.2 13.0 all-to-all-start
  5922.3 16.0 all-to-all-done
  5960.9 711.3 %all-gather.6.cloned.1.call-done = f32[256,1,5376]{2,1,0:T(1,128)} async-done(((f32[1,1,5376]{2,1,0:T(1,128)}), f32[256,1,5376]{2,1,0:T(1,128)}) %all-gather.6.cloned.1.call-update) | async-done | bytes 5505040 | tf_op jit(solution)/shard_map/while/body/eval_jaxpr/all_gather | solution.py:108
  6714.9 11.9 while.22
  6740.4 13.0 all-to-all-start
  6753.6 16.0 all-to-all-done
  6792.2 711.3 %all-gather.6.cloned.1.call-done = f32[256,1,5376]{2,1,0:T(1,128)} async-done(((f32[1,1,5376]{2,1,0:T(1,128)}), f32[256,1,5376]{2,1,0:T(1,128)}) %all-gather.6.cloned.1.call-update) | async-done | bytes 5505040 | tf_op jit(solution)/shard_map/while/body/eval_jaxpr/all_gather | solution.py:108
  7546.2 11.9 while.22
  7571.7 13.0 all-to-all-start
  7584.8 16.0 all-to-all-done
  7623.4 711.3 %all-gather.6.cloned.1.call-done = f32[256,1,5376]{2,1,0:T(1,128)} async-done(((f32[1,1,5376]{2,1,0:T(1,128)}), f32[256,1,5376]{2,1,0:T(1,128)}) %all-gather.6.cloned.1.call-update) | async-done | bytes 5505040 | tf_op jit(solution)/shard_map/while/body/eval_jaxpr/all_gather | solution.py:108
  (826 shorter events, 855.6 us)
Async XLA Ops:
  42.5 14.2 collective-permute-start
  49.4 16.2 collective-permute-start.1
  92.4 29.2 all-to-all-start
  103.5 750.0 %all-gather.6.cloned.1.call-start = ((), (), s32[]{:S(2)}) async-start(), calls=%async_computation.1 | async-start | bytes 5526528 | tf_op jit(solution)/shard_map/while/body/eval_jaxpr/all_gather | solution.py:108
  132.5 9.8 copy-start
  879.5 12.0 collective-permute-start
  879.6 15.3 collective-permute-start.1
  921.6 29.2 all-to-all-start
  934.6 750.0 %all-gather.6.cloned.1.call-start = ((), (), s32[]{:S(2)}) async-start(), calls=%async_computation.1 | async-start | bytes 5526528 | tf_op jit(solution)/shard_map/while/body/eval_jaxpr/all_gather | solution.py:108
  961.6 9.8 copy-start
  1710.7 12.1 collective-permute-start
  1710.8 15.3 collective-permute-start.1
  1752.8 29.2 all-to-all-start
  1765.9 750.0 %all-gather.6.cloned.1.call-start = ((), (), s32[]{:S(2)}) async-start(), calls=%async_computation.1 | async-start | bytes 5526528 | tf_op jit(solution)/shard_map/while/body/eval_jaxpr/all_gather | solution.py:108
  1792.9 9.8 copy-start
  2542.0 10.3 collective-permute-start
  2542.1 15.3 collective-permute-start.1
  2584.1 29.2 all-to-all-start
  2597.1 750.0 %all-gather.6.cloned.1.call-start = ((), (), s32[]{:S(2)}) async-start(), calls=%async_computation.1 | async-start | bytes 5526528 | tf_op jit(solution)/shard_map/while/body/eval_jaxpr/all_gather | solution.py:108
  2624.1 9.8 copy-start
  3373.2 12.1 collective-permute-start
  3373.3 15.3 collective-permute-start.1
  3415.3 27.9 all-to-all-start
  3427.8 750.7 %all-gather.6.cloned.1.call-start = ((), (), s32[]{:S(2)}) async-start(), calls=%async_computation.1 | async-start | bytes 5526528 | tf_op jit(solution)/shard_map/while/body/eval_jaxpr/all_gather | solution.py:108
  3454.1 9.8 copy-start
  4204.6 12.0 collective-permute-start
  4204.7 15.3 collective-permute-start.1
  4246.7 29.2 all-to-all-start
  4259.7 750.0 %all-gather.6.cloned.1.call-start = ((), (), s32[]{:S(2)}) async-start(), calls=%async_computation.1 | async-start | bytes 5526528 | tf_op jit(solution)/shard_map/while/body/eval_jaxpr/all_gather | solution.py:108
  5035.8 12.0 collective-permute-start
  5035.9 15.3 collective-permute-start.1
  5077.9 29.2 all-to-all-start
  5091.0 750.0 %all-gather.6.cloned.1.call-start = ((), (), s32[]{:S(2)}) async-start(), calls=%async_computation.1 | async-start | bytes 5526528 | tf_op jit(solution)/shard_map/while/body/eval_jaxpr/all_gather | solution.py:108
  5118.0 9.8 copy-start
  5867.1 12.0 collective-permute-start
  5867.2 15.3 collective-permute-start.1
  5909.2 29.2 all-to-all-start
  5922.2 750.0 %all-gather.6.cloned.1.call-start = ((), (), s32[]{:S(2)}) async-start(), calls=%async_computation.1 | async-start | bytes 5526528 | tf_op jit(solution)/shard_map/while/body/eval_jaxpr/all_gather | solution.py:108
  6698.3 12.0 collective-permute-start
  6698.4 15.3 collective-permute-start.1
  6740.4 29.2 all-to-all-start
  6753.5 750.0 %all-gather.6.cloned.1.call-start = ((), (), s32[]{:S(2)}) async-start(), calls=%async_computation.1 | async-start | bytes 5526528 | tf_op jit(solution)/shard_map/while/body/eval_jaxpr/all_gather | solution.py:108
  6780.5 9.8 copy-start
  7529.6 12.0 collective-permute-start
  7529.7 15.3 collective-permute-start.1
  7571.7 29.2 all-to-all-start
  7584.7 750.0 %all-gather.6.cloned.1.call-start = ((), (), s32[]{:S(2)}) async-start(), calls=%async_computation.1 | async-start | bytes 5526528 | tf_op jit(solution)/shard_map/while/body/eval_jaxpr/all_gather | solution.py:108
  7611.7 9.8 copy-start
  (9 other events, 53.5 us)
Sparse Core Ops, SparseCore 0:
  143.6 709.7 all-gather.5
  972.8 711.8 all-gather.5
  1804.0 711.8 all-gather.5
  2635.3 711.8 all-gather.5
  3465.3 713.2 all-gather.5
  4297.9 711.8 all-gather.5
  5129.1 711.8 all-gather.5
  5960.4 711.8 all-gather.5
  6791.6 711.8 all-gather.5
  7622.9 711.8 all-gather.5
